TPU v7x, 128 devices: a whole 4x4x4 slice. The times are simulated.
128 devices in a mesh: ctx: 16 (over x, y_lo, core), head: 8 (over z, y_hi).
Axes of the slice: x: 4, y: 4 (y_hi: 2, y_lo: 2; y = y_hi * 2 + y_lo), z: 4, core: 2. Of those that a mesh axis runs over, the one named last changes fastest.
Arguments:
- hidden: bfloat16 [32768, 1024], P('ctx'), may hold values from -6 to 6
- norm_gain: float32 [1024], replicated, may hold values from 0.1 to 1.9
- w_zx: bfloat16 [1024, 2, 2048], P(None, None, 'head'), may hold values from -0.1875 to 0.1875
- w_bc: bfloat16 [1024, 256], replicated, may hold values from -0.1875 to 0.1875
- w_dt: bfloat16 [1024, 32], P(None, 'head'), may hold values from -0.1875 to 0.1875
- dt_bias: float32 [32], P('head'), may hold values from -2 to 1
- decay_rate: float32 [32], P('head'), may hold values from 1e-07 to 0.03
- skip_gain: float32 [32], P('head'), may hold values from 0.5 to 2
- conv_x: float32 [4, 2048], P(None, 'head'), may hold values from -3 to 3
- conv_bc: float32 [4, 256], replicated, may hold values from -3 to 3
- w_out: bfloat16 [2048, 1024], P('head'), may hold values from -0.125 to 0.125
Outputs:
- mixed: bfloat16 [32768, 1024], P(('ctx', 'head'))
All inputs are finite; a program needn't handle non-finite values.
Results may differ from a plain program's by a relative error of at most 0.013.
Values may be sent and summed in bfloat16 or wider, within the bound.
A program may use at most 128 MiB of HBM per device.

v0:
```python
import jax
import jax.numpy as jnp
from jax import lax
from jax.experimental import pallas as pl
from jax.experimental.pallas import tpu as pltpu
from jax.sharding import PartitionSpec as P

MESH = pl.DeviceIdType.MESH
F32 = jnp.float32
BF16 = jnp.bfloat16
BLOCK = 256
STATE = 128
HEAD = 64
CTX = 16
GROUP = 8
STAGES = 4
MESSAGE = STATE + 16
LOG2E = 1.4426950408889634
epsilon = 1e-05


def dot(a, b):
    return jnp.dot(a, b, preferred_element_type=F32)


def dot_rows(a, b):
    return lax.dot_general(a, b, (((1,), (1,)), ((), ())), preferred_element_type=F32)


def halves(v):
    high = v.astype(BF16)
    return high, (v - high.astype(F32)).astype(BF16)


def silu(v):
    half = 0.5 * v
    return half + half * jnp.tanh(half)


def softplus(v):
    return jnp.maximum(v, 0.0) + jnp.log1p(jnp.exp(-jnp.abs(v)))


def iotas(shape):
    return lax.broadcasted_iota(jnp.int32, shape, 0), lax.broadcasted_iota(jnp.int32, shape, 1)


def remote(src, dst, send, recv, ctx, head):
    return pltpu.make_async_remote_copy(
        src_ref=src, dst_ref=dst, send_sem=send, recv_sem=recv,
        device_id=(ctx, head), device_id_type=MESH,
    )


def kernel(
    hid, gain, wzx, wbc, wdt, consts, conv, wout, out,
    hbuf, wX, wZ, wo, st, scl, dtb, vb, wb, btb, cb, cum, ec, ent, prow, ins, gb,
    state, arow, xs, xa, msg, rmsg, cbuf, rbuf, acc, low, upp, spread, mean, flip,
    hsem, osem, wsend, wrecv, halo_send, halo_recv, ssend, srecv, csend, crecv,
):
    blocks = hbuf.shape[0]
    inner = vb.shape[3]
    heads = inner // HEAD
    width = inner + 2 * STATE
    ctx = lax.axis_index("ctx")
    me = lax.axis_index("head")
    core = lax.rem(ctx, 2)

    barrier = pltpu.get_barrier_semaphore()
    ctx_peers = [lax.rem(ctx + 1, CTX), lax.rem(ctx + CTX - 1, CTX)]
    for k in range(STAGES):
        bit = lax.rem(lax.div(ctx, 2**k), 2)
        ctx_peers.append(ctx + (1 - 2 * bit) * 2**k)
    head_peers = [lax.rem(me + d, GROUP) for d in range(1, GROUP)]
    for peer in ctx_peers:
        pl.semaphore_signal(barrier, inc=1, device_id=(peer, me), device_id_type=MESH)
    for peer in head_peers:
        pl.semaphore_signal(barrier, inc=1, device_id=(ctx, peer), device_id_type=MESH)

    def load(b):
        return pltpu.make_async_copy(
            hid.at[pl.ds(pl.multiple_of(b * BLOCK, BLOCK), BLOCK), :], hbuf.at[b], hsem.at[b]
        )

    for b in (blocks - 1, *range(blocks - 1)):
        load(b).start()
    own = [
        pltpu.make_async_copy(wout.at[pl.ds(c * 128, 128), :], wo.at[me, c], osem.at[c])
        for c in range(2)
    ]
    for c in range(2):
        own[c].start()

    r0, c0 = iotas((BLOCK, BLOCK))
    low[...] = (r0 >= c0).astype(BF16)
    upp[...] = (r0 <= c0).astype(BF16)
    flip[...] = (r0 + c0 == BLOCK - 1).astype(BF16)
    lane_head = c0 // HEAD
    q0 = lax.rem(r0, 128)
    for s in range(2):
        spread[s] = (q0 == lane_head + s * heads).astype(BF16)
    mean[...] = jnp.where(r0 // HEAD == lane_head, 1.0 / HEAD, 0.0).astype(BF16)

    pieces = wX.shape[0] // BLOCK
    for j in range(pieces):
        span = pl.ds(j * BLOCK, BLOCK)
        back = pl.ds((pieces - 1 - j) * BLOCK, BLOCK)
        column = jnp.concatenate(
            [
                jnp.broadcast_to(gain[pl.ds(2 * j + t, 1), :], (128, 128)).T
                for t in range(2)
            ],
            axis=0,
        )
        gz = (wzx[span, :].astype(F32) * jnp.concatenate([column] * 4, axis=1)).astype(BF16)
        gbc = (wbc[span, :].astype(F32) * jnp.concatenate([column] * 2, axis=1)).astype(BF16)
        gdt = (wdt[span, :].astype(F32) * column).astype(BF16)
        gx = jnp.concatenate([gz[:, inner:], gbc], axis=1)
        turned = dot(flip[...], jnp.concatenate([gx, gz[:, :inner], gdt], axis=1)).astype(BF16)
        wX[span, :width] = gx
        wX[back, width : 2 * width] = turned[:, :width]
        wZ[span, :inner] = gz[:, :inner]
        wZ[back, inner:] = turned[:, width : width + inner]
        mine = lax.broadcasted_iota(jnp.int32, gdt.shape, 1) < heads
        zero = jnp.zeros_like(gdt)
        dtb[j] = jnp.where(mine, gdt, zero).astype(F32)
        scl[pieces - 1 - j] = jnp.where(mine, zero, turned[:, width + inner :]).astype(F32)
    for j in range(pieces):
        wX[pl.ds(j * BLOCK, BLOCK), 2 * width :] = (dtb[j] + scl[j]).astype(BF16)

    pl.semaphore_wait(barrier, len(ctx_peers) + len(head_peers))

    partner = ctx_peers[2]
    across = me + 1 - 2 * lax.rem(me, 2)
    up = lax.rem(me + 2, GROUP)
    down = lax.rem(me + GROUP - 2, GROUP)
    onward = lax.rem(me + 2 + core * 4, GROUP)
    origin = lax.rem(me + 6 - core * 4, GROUP)

    def other(h):
        return h + 1 - 2 * lax.rem(h, 2)

    far = lax.rem(me + 4, GROUP)
    mine_half = wout.at[pl.ds(pl.multiple_of(core * 128, 128), 128), :]
    sources = [across, down, up, other(down), other(up), far, other(far)]

    def slot_copy(src, k, source_here, ctx_to, head_to, send_index):
        return remote(src, wo.at[source_here, core], wsend.at[send_index], wrecv.at[k], ctx_to, head_to)

    w1 = [
        slot_copy(mine_half, 0, me, ctx, across, 0),
        slot_copy(mine_half, 1, me, ctx, up, 1),
        slot_copy(mine_half, 2, me, ctx, down, 2),
    ]
    w2 = [
        slot_copy(wo.at[across, core], 3, across, ctx, up, 3),
        slot_copy(wo.at[across, core], 4, across, ctx, down, 4),
    ]
    w3 = [
        slot_copy(wo.at[origin, core], 5, origin, ctx, onward, 5),
        slot_copy(wo.at[other(origin), core], 6, other(origin), ctx, onward, 6),
    ]
    w4 = [
        remote(wo.at[h, core], wo.at[h, core], wsend.at[7 + k], wrecv.at[7 + k], partner, me)
        for k, h in enumerate(sources)
    ]

    def arrived(k):
        remote(mine_half, wo.at[sources[k], core], wsend.at[0], wrecv.at[k], ctx, me).wait_recv()

    def partner_arrived(k):
        h = sources[k]
        remote(wo.at[h, core], wo.at[h, 1 - core], wsend.at[0], wrecv.at[7 + k], partner, me).wait_recv()

    for copy in w1:
        copy.start()

    rate = consts[1:2, :128]
    bias = consts[0:1, :128]
    skip = consts[2:3, :]

    def first_rows():
        return [
            remote(
                st.at[0, blocks, pl.ds(0, 8), :], st.at[0, 0, pl.ds(0, 8), :],
                halo_send.at[0], halo_recv.at[0], ctx_peers[0], me,
            ),
            remote(
                st.at[1, 0, pl.ds(BLOCK, 8), :], st.at[1, blocks, pl.ds(BLOCK, 8), :],
                halo_send.at[1], halo_recv.at[1], ctx_peers[1], me,
            ),
        ]

    def project(i, carry):
        b = lax.rem(i + blocks - 1, blocks)
        load(b).wait()
        h = hbuf[b]
        hf = h.astype(F32)
        scale = lax.rsqrt(jnp.sum(hf * hf, axis=1, keepdims=True) / h.shape[1] + epsilon)
        p = dot(h, wX[...])
        ahead = p[:, :width] * scale
        st[0, b, 8:, :] = ahead
        st[0, b + 1, 0:8, :] = ahead[BLOCK - 8 :, :]
        behind = p[:, width : 2 * width] * scale
        st[1, b + 1, :BLOCK, :] = behind
        st[1, b, BLOCK:, :] = behind[0:8, :]
        dtb[b] = softplus(p[:, 2 * width :] * scale + bias)
        scl[b] = jnp.broadcast_to(scale, (BLOCK, 128))

        @pl.when(i == 2)
        def _():
            for copy in first_rows():
                copy.start()

        return carry

    lax.fori_loop(0, blocks, project, 0)

    arrived(0)
    for copy in w2:
        copy.start()
    w4[0].start()

    for copy in first_rows():
        copy.wait_recv()
    st[0, 0, 0:8, :] = jnp.where(ctx == 0, 0.0, st[0, 0, 0:8, :])
    st[1, blocks, BLOCK:, :] = jnp.where(ctx == CTX - 1, 0.0, st[1, blocks, BLOCK:, :])

    state[...] = jnp.zeros_like(state)
    arow[...] = jnp.ones_like(arow)

    def local(i, carry):
        for s in range(2):
            b = i if s == 0 else blocks - 1 - i
            total = jnp.zeros((BLOCK, width), F32)
            for k in range(4):
                shift = 5 + k if s == 0 else 3 - k
                total = total + conv[k : k + 1, :] * st[s, b + s, shift : shift + BLOCK, :]
            active = silu(total)
            x = active[:, :inner]
            bt = active[:, inner : inner + STATE].T.astype(BF16)
            btb[s, b] = bt
            cb[s, b] = active[:, inner + STATE :].astype(BF16)
            vb[s, b] = x.astype(BF16)
            dt = dtb[b]
            high, rest = halves(dt * (-LOG2E * rate))
            tri = low[...] if s == 0 else upp[...]
            c = dot(tri, high) + dot(tri, rest)
            cum[s, b] = c
            end = c[BLOCK - 1 : BLOCK, :] if s == 0 else c[0:1, :]
            table = spread[s]
            steps = dot(jnp.concatenate(halves(dt), axis=1), table)
            late = dot(jnp.concatenate(halves(dt * jnp.exp2(end - c)), axis=1), table)
            reach = dot(jnp.concatenate(halves(jnp.exp2(c)), axis=1), table)
            wb[s, b] = (x * steps).astype(BF16)
            ec[s, b] = reach
            ends = dot(bt, (x * late).astype(BF16))
            decay = reach[BLOCK - 1 : BLOCK, :] if s == 0 else reach[0:1, :]
            held = state[s]
            ent[s, b] = held
            state[s] = decay * held + ends
            before = arow[s, 0:1, :]
            prow[s, b] = jnp.broadcast_to(before, (8, inner))
            arow[s] = jnp.broadcast_to(before * decay, (8, inner))
        return carry

    lax.fori_loop(0, blocks, local, 0)

    xs[...] = jnp.zeros_like(xs)
    xa[...] = jnp.ones_like(xa)

    line = lax.broadcasted_iota(jnp.int32, (16, inner), 0)

    def exchange(k):
        return remote(
            msg.at[k], rmsg.at[k], ssend.at[k], srecv.at[k], ctx_peers[2 + k], me
        )

    def send_stage(k):
        for s in range(2):
            msg[k, s, :STATE, :] = state[s].astype(BF16)
            high, rest = halves(arow[s, 0:1, :])
            msg[k, s, STATE:, :] = jnp.where(
                line == 0, high.astype(F32), jnp.where(line == 1, rest.astype(F32), 0.0)
            ).astype(BF16)
        exchange(k).start()

    def merge_stage(k):
        exchange(k).wait_recv()
        bit = lax.rem(lax.div(ctx, 2**k), 2)
        for s in range(2):
            theirs = rmsg[k, s, :STATE, :].astype(F32)
            tail = rmsg[k, s, STATE:, :].astype(F32)
            factor = tail[0:1, :] + tail[1:2, :]
            earlier = bit == 1 - s
            now = state[s]
            mine = arow[s, 0:1, :]
            reach = xa[s, 0:1, :]
            xs[s] = jnp.where(earlier, reach * theirs + xs[s], xs[s])
            xa[s] = jnp.broadcast_to(jnp.where(earlier, reach * factor, reach), (8, inner))
            state[s] = jnp.where(earlier, mine * theirs + now, factor * now + theirs)
            arow[s] = jnp.broadcast_to(mine * factor, (8, inner))

    send_stage(0)

    for k in (1, 2):
        arrived(k)
        w4[k].start()
    arrived(3)
    arrived(4)
    for copy in w3:
        copy.start()
    w4[3].start()
    w4[4].start()

    def within(i, carry):
        for k in range(STAGES - 1):

            @pl.when(i == 2 * k + 2)
            def _():
                merge_stage(k)
                send_stage(k + 1)

        h = hbuf[i]
        scale = scl[i]
        g = silu(dot(h, wZ[...]) * jnp.concatenate([scale] * (2 * inner // 128), axis=1))
        first, second = iotas((BLOCK, BLOCK))
        side = lax.broadcasted_iota(jnp.int32, (BLOCK, 128), 1) < HEAD
        for s in range(2):
            gb[s, i] = g[:, s * inner : (s + 1) * inner]
            keep = first >= second if s == 0 else first <= second
            scores = jnp.where(keep, dot(cb[s, i], btb[s, i]), 0.0)
            c = cum[s, i]
            turned = c.T
            for pair in range(heads // 2):
                parts = []
                for t in range(2):
                    lane = s * heads + pair * 2 + t
                    gap = c[:, lane : lane + 1] - turned[lane : lane + 1, :]
                    mixing = (scores * jnp.exp2(jnp.minimum(gap, 0.0))).astype(BF16)
                    parts.append(dot(mixing, wb[s, i, :, pair * 128 : (pair + 1) * 128]))
                at = slice(pair * 128, (pair + 1) * 128)
                ins[s, i, :, at] = jnp.where(side, parts[0], parts[1]) + skip[:, at] * vb[
                    s, i, :, at
                ].astype(F32)
        return carry

    lax.fori_loop(0, blocks, within, 0)
    merge_stage(STAGES - 1)

    for k in (5, 6):
        arrived(k)
        w4[k].start()

    def finish(i, carry):
        b = lax.rem(me + 1 + i, blocks)
        both = jnp.zeros((BLOCK, inner), F32)
        for s in range(2):
            whole = (ent[s, b] + prow[s, b][0:1, :] * xs[s]).astype(BF16)
            result = ins[s, b] + ec[s, b] * dot(cb[s, b], whole)
            gated = result * gb[s, b]
            power = dot((gated * gated).astype(BF16), mean[...])
            both = both + gated * lax.rsqrt(power + epsilon)
        cbuf[b] = both.astype(BF16)

        @pl.when(i < blocks - 1)
        def _():
            remote(cbuf.at[b], rbuf.at[me], csend.at[b], crecv.at[me], ctx, b).start()

        return carry

    lax.fori_loop(0, blocks, finish, 0)

    for c in range(2):
        own[c].wait()
    for k in range(7):
        partner_arrived(k)

    acc[...] = hbuf[me].astype(F32)

    def multiply(block, j):
        for c in range(2):
            acc[...] += dot(block[:, c * 128 : (c + 1) * 128], wo[j, c])

    multiply(cbuf[me], me)

    def gathered(i, carry):
        j = lax.rem(me + blocks - 1 - i, blocks)
        remote(cbuf.at[j], rbuf.at[j], csend.at[j], crecv.at[j], ctx, j).wait_recv()
        multiply(rbuf[j], j)
        return carry

    lax.fori_loop(0, blocks - 1, gathered, 0)
    out[...] = acc[...].astype(BF16)

    for copy in w1 + w2 + w3 + w4 + first_rows() + [exchange(k) for k in range(STAGES)]:
        copy.wait_send()

    def drained(i, carry):
        j = lax.rem(me + 1 + i, blocks)
        remote(cbuf.at[j], rbuf.at[me], csend.at[j], crecv.at[me], ctx, j).wait_send()
        return carry

    lax.fori_loop(0, blocks - 1, drained, 0)


def on_device(
    hidden, norm_gain, w_zx, w_bc, w_dt, dt_bias, decay_rate, skip_gain, conv_x, conv_bc, w_out
):
    amount, wide = hidden.shape
    inner = conv_x.shape[1]
    heads = w_dt.shape[1]
    width = inner + 2 * STATE
    blocks = amount // BLOCK
    pad = [(0, inner - 2 * heads)]
    consts = jnp.stack(
        [
            jnp.pad(jnp.tile(dt_bias, 2), pad[0]),
            jnp.pad(jnp.tile(decay_rate, 2), pad[0]),
            jnp.repeat(skip_gain, HEAD),
        ]
    )
    wdt = jnp.pad(jnp.concatenate([w_dt, w_dt], axis=1), [(0, 0), (0, 128 - 2 * heads)])
    conv = jnp.concatenate([conv_x, conv_bc], axis=1)
    vmem = pl.BlockSpec(memory_space=pltpu.VMEM)
    hbm = pl.BlockSpec(memory_space=pl.ANY)
    dma = pltpu.SemaphoreType.DMA
    return pl.pallas_call(
        kernel,
        out_shape=jax.ShapeDtypeStruct((BLOCK, wide), BF16),
        in_specs=[hbm, vmem, vmem, vmem, vmem, vmem, vmem, hbm],
        out_specs=vmem,
        scratch_shapes=[
            pltpu.VMEM((blocks, BLOCK, wide), BF16),
            pltpu.VMEM((wide, 2 * width + 128), BF16),
            pltpu.VMEM((wide, 2 * inner), BF16),
            pltpu.VMEM((GROUP, 2, 128, wide), BF16),
            pltpu.VMEM((2, blocks + 1, BLOCK + 8, width), F32),
            pltpu.VMEM((blocks, BLOCK, 128), F32),
            pltpu.VMEM((blocks, BLOCK, 128), F32),
            pltpu.VMEM((2, blocks, BLOCK, inner), BF16),
            pltpu.VMEM((2, blocks, BLOCK, inner), BF16),
            pltpu.VMEM((2, blocks, STATE, BLOCK), BF16),
            pltpu.VMEM((2, blocks, BLOCK, STATE), BF16),
            pltpu.VMEM((2, blocks, BLOCK, 128), F32),
            pltpu.VMEM((2, blocks, BLOCK, inner), F32),
            pltpu.VMEM((2, blocks, STATE, inner), F32),
            pltpu.VMEM((2, blocks, 8, inner), F32),
            pltpu.VMEM((2, blocks, BLOCK, inner), F32),
            pltpu.VMEM((2, blocks, BLOCK, inner), F32),
            pltpu.VMEM((2, STATE, inner), F32),
            pltpu.VMEM((2, 8, inner), F32),
            pltpu.VMEM((2, STATE, inner), F32),
            pltpu.VMEM((2, 8, inner), F32),
            pltpu.VMEM((STAGES, 2, MESSAGE, inner), BF16),
            pltpu.VMEM((STAGES, 2, MESSAGE, inner), BF16),
            pltpu.VMEM((GROUP, BLOCK, inner), BF16),
            pltpu.VMEM((GROUP, BLOCK, inner), BF16),
            pltpu.VMEM((BLOCK, wide), F32),
            pltpu.VMEM((BLOCK, BLOCK), BF16),
            pltpu.VMEM((BLOCK, BLOCK), BF16),
            pltpu.VMEM((2, BLOCK, BLOCK), BF16),
            pltpu.VMEM((BLOCK, BLOCK), BF16),
            pltpu.VMEM((BLOCK, BLOCK), BF16),
            dma((blocks,)),
            dma((2,)),
            dma((14,)),
            dma((14,)),
            dma((2,)),
            dma((2,)),
            dma((STAGES,)),
            dma((STAGES,)),
            dma((GROUP,)),
            dma((GROUP,)),
        ],
        compiler_params=pltpu.CompilerParams(
            collective_id=0, has_side_effects=True, vmem_limit_bytes=63 * 1024 * 1024
        ),
    )(
        hidden,
        norm_gain.reshape(8, wide // 8),
        w_zx.reshape(wide, 2 * inner),
        w_bc,
        wdt,
        consts,
        conv,
        w_out,
    )


def solution(mesh):
    placed = (
        P("ctx", None),
        P(),
        P(None, None, "head"),
        P(),
        P(None, "head"),
        P("head"),
        P("head"),
        P("head"),
        P(None, "head"),
        P(),
        P("head", None),
    )
    return jax.shard_map(
        on_device, mesh=mesh, in_specs=placed, out_specs=P(("ctx", "head"), None), check_vma=False
    )
```

profile of v0, /device:TPU:0, one launch (start us, length us, event | category | flops | bytes accessed | tf_op | source)
XLA Modules:
  0.0 73.3 jit_solution(136397162322767355)
XLA Ops:
  0.0 0.7 tile.8
  0.7 0.1 tile.9
  0.7 0.7 tile.20
  1.4 0.1 tile.21
  1.5 0.7 broadcast_in_dim.3
  2.2 0.1 stack_reshape.3
  2.3 0.6 pad_maximum_fusion.2.consts
  2.9 1.3 %pad_maximum_fusion.1.conv = f32[4,512]{1,0:T(4,128)} fusion(f32[4,256]{1,0:T(4,128)} %param.20, f32[4,256]{1,0:T(4,128)} %param.19), kind=kLoop, calls=%fused_computation.1 | loop fusion | flops 2048 | bytes 16384 | tf_op jit(solution)/shard_map/concatenate | solution.py:424
  4.2 0.8 %pad_maximum_fusion = bf16[1024,8]{0,1:T(8,128)(2,1)S(1)} fusion(bf16[1024,4]{0,1:T(4,128)(2,1)} %param.15), kind=kLoop, calls=%fused_computation | loop fusion | flops 32768 | bytes 24576 | tf_op jit(solution)/shard_map/concatenate | solution.py:423
  5.0 0.2 copy.14
  5.2 0.8 %pad.11.wdt = bf16[1024,128]{1,0:T(8,128)(2,1)} pad(bf16[1024,8]{1,0:T(8,128)(2,1)S(1)} %copy.14, bf16[]{:T(256)} %constant.3.clone.1), padding=0_0x0_120 | pad | bytes 278530 | tf_op jit(solution)/shard_map/jit(_pad)/pad | solution.py:423
  5.9 2.4 %copy.15 = bf16[128,8,2,256]{3,1,2,0:T(8,128)(2,1)} copy(bf16[128,8,2,256]{3,2,1,0:T(2,128)(2,1)} %bitcast.6) | data formatting | bytes 2097152
  8.4 63.1 %shard_map.109 = bf16[256,1024]{1,0:T(8,128)(2,1)} custom-call(bf16[2048,1024]{1,0:T(8,128)(2,1)} %hid.1, f32[8,128]{1,0:T(8,128)} %bitcast.7, bf16[1024,512]{1,0:T(8,128)(2,1)} %bitcast.5, bf16[1024,256]{1,0:T(8,128)(2,1)} %wbc.1, bf16[1024,128]{1,0:T(8,128)(2,1)} %pad.11.wdt, f32[3,256]{1,0:T(4,128)} %pad_maximum_fusion.2.consts, ...), custom_call_target="tpu_custom_call" | custom-call | tf_op jit(solution)/shard_map/pallas_call | solution.py:428
  71.4 1.9 %copy.17 = bf16[256,1024]{1,0:T(8,128)(2,1)} copy(bf16[256,1024]{1,0:T(8,128)(2,1)} %shard_map.109) | data formatting | bytes 1048576
  (2 shorter events, 0.0 us)
where the time goes:
time: 73.6 us; the launch traced here: 73.3 us
  Pallas kernels  63.1 us (86%)
  local copies, waits for them, and re-layouts  7.54 us (10%)
  other arithmetic  2.69 us (4%)
    pallas_call x1, Pallas kernels, on_device(): pl.pallas_call(kernel, out_shape=jax.ShapeDtypeStruct((BLOCK, wide), BF16...  63.1 us
    unnamed x2, local copies, waits for them, and re-layouts  4.31 us

commit v1 on v0

v1 whole, which is shorter than its diff:
```python
import jax
import jax.numpy as jnp
from jax import lax
from jax.experimental import pallas as pl
from jax.experimental.pallas import tpu as pltpu
from jax.sharding import PartitionSpec as P

MESH = pl.DeviceIdType.MESH
F32 = jnp.float32
BF16 = jnp.bfloat16
BLOCK = 256
STATE = 128
HEAD = 64
CTX = 16
GROUP = 8
MESSAGE = STATE + 16
LOG2E = 1.4426950408889634
epsilon = 1e-05


def dot(a, b):
    return jnp.dot(a, b, preferred_element_type=F32)


def dot_rows(a, b):
    return lax.dot_general(a, b, (((1,), (1,)), ((), ())), preferred_element_type=F32)


def halves(v):
    high = v.astype(BF16)
    return high, (v - high.astype(F32)).astype(BF16)


def silu(v):
    half = 0.5 * v
    return half + half * jnp.tanh(half)


def softplus(v):
    return jnp.maximum(v, 0.0) + jnp.log1p(jnp.exp(-jnp.abs(v)))


def iotas(shape):
    return lax.broadcasted_iota(jnp.int32, shape, 0), lax.broadcasted_iota(jnp.int32, shape, 1)


def remote(src, dst, send, recv, ctx, head):
    return pltpu.make_async_remote_copy(
        src_ref=src, dst_ref=dst, send_sem=send, recv_sem=recv,
        device_id=(ctx, head), device_id_type=MESH,
    )


def kernel(
    hid, gain, wzx_hbm, wbc_hbm, wdt, bias_in, rate_in, skip_in, conv_x, conv_bc, wout, out,
    hbuf, wX, wZ, wo, st, scl, dtb, vb, btb, cb, cum, ec, ent, prow, ins,
    state, arow, xs, xa, msg, rmsg, cbuf, rbuf, acc, low, upp, spread, mean, flip, wzx, wbc, skips, wC, sc,
    hs, ha, ys, ya, hmsg, hrmsg, xmsg, fmsg, frmsg, wsem, hsem, osem, wsend, wrecv, halo_send, halo_recv, ssend, srecv, csend, crecv,
):
    blocks = hbuf.shape[0]
    inner = vb.shape[3]
    heads = inner // HEAD
    width = inner + STATE
    ctx = lax.axis_index("ctx")
    me = lax.axis_index("head")
    core = lax.rem(ctx, 2)

    barrier = pltpu.get_barrier_semaphore()
    ctx_peers = [lax.rem(ctx + 1, CTX), lax.rem(ctx + CTX - 1, CTX)]
    for k in range(2):
        bit = lax.rem(lax.div(ctx, 2**k), 2)
        ctx_peers.append(ctx + (1 - 2 * bit) * 2**k)
    ctx_peers.extend(lax.rem(ctx + 4 * d, CTX) for d in range(1, 4))
    head_peers = [lax.rem(me + d, GROUP) for d in range(1, GROUP)]
    for peer in ctx_peers:
        pl.semaphore_signal(barrier, inc=1, device_id=(peer, me), device_id_type=MESH)
    for peer in head_peers:
        pl.semaphore_signal(barrier, inc=1, device_id=(ctx, peer), device_id_type=MESH)

    def load(b):
        return pltpu.make_async_copy(
            hid.at[pl.ds(pl.multiple_of(b * BLOCK, BLOCK), BLOCK), :], hbuf.at[b], hsem.at[b]
        )

    weights = [
        pltpu.make_async_copy(wzx_hbm, wzx, wsem.at[0]),
        pltpu.make_async_copy(wbc_hbm, wbc, wsem.at[1]),
    ]
    for copy in weights:
        copy.start()
    for b in (blocks - 1, *range(blocks - 1)):
        load(b).start()
    own = pltpu.make_async_copy(wout, wo.at[me], osem.at[0])
    own.start()

    r0, c0 = iotas((BLOCK, BLOCK))
    low[...] = (r0 >= c0).astype(BF16)
    upp[...] = (r0 <= c0).astype(BF16)
    flip[...] = (r0 + c0 == BLOCK - 1).astype(BF16)
    lane_head = c0 // HEAD
    q0 = lax.rem(r0, 128)
    for s in range(2):
        spread[s] = (q0 == lane_head + s * heads).astype(BF16)
    mean[...] = jnp.where(r0 // HEAD == lane_head, 1.0 / HEAD, 0.0).astype(BF16)

    lane = lax.broadcasted_iota(jnp.int32, (1, 128), 1)
    wide_lane = lax.broadcasted_iota(jnp.int32, (1, inner), 1)
    rate = jnp.zeros((1, 128), F32)
    bias = jnp.zeros((1, 128), F32)
    skip = jnp.zeros((1, inner), F32)
    for h in range(heads):
        taken = (lane == h) | (lane == heads + h)
        rate = jnp.where(taken, rate_in[h] * (-LOG2E), rate)
        bias = jnp.where(taken, bias_in[h], bias)
        skip = jnp.where(wide_lane // HEAD == h, skip_in[h], skip)
    skips[...] = jnp.broadcast_to(skip, skips.shape)

    acc[0:128, :] = jnp.zeros((128, acc.shape[1]), F32)
    pieces = wX.shape[0] // BLOCK
    for copy in weights:
        copy.wait()

    def prepare(j, carry):
        span = pl.ds(pl.multiple_of(j * BLOCK, BLOCK), BLOCK)
        back = pl.ds(pl.multiple_of((pieces - 1 - j) * BLOCK, BLOCK), BLOCK)
        lines = [gain[pl.ds(2 * j + t, 1), :] for t in range(2)]
        column = jnp.concatenate(
            [jnp.broadcast_to(line, (128, 128)).T for line in lines], axis=0
        )
        gz = (wzx[span, :].astype(F32) * jnp.concatenate([column] * 4, axis=1)).astype(BF16)
        gbc = (wbc[span, :].astype(F32) * jnp.concatenate([column] * 2, axis=1)).astype(BF16)
        gx = jnp.concatenate([gz[:, inner:], gbc], axis=1)
        turned = dot(flip[...], jnp.concatenate([gx, gz[:, :inner]], axis=1)).astype(BF16)
        wX[span, :width] = gx[:, :width]
        wX[back, width : 2 * width] = turned[:, :width]
        wC[span, :STATE] = gx[:, width:]
        wC[back, STATE:] = turned[:, width : width + STATE]
        wZ[span, :inner] = gz[:, :inner]
        wZ[back, inner:] = turned[:, width + STATE :]
        gdt = (wdt[:, span].astype(F32) * jnp.concatenate(lines, axis=1)).astype(BF16)
        acc[0:heads, span] = gdt.astype(F32)
        acc[heads : 2 * heads, back] = dot(gdt, flip[...])
        return carry

    lax.fori_loop(0, pieces, prepare, 0)
    for j in range(wX.shape[0] // 128):
        span = slice(j * 128, (j + 1) * 128)
        wX[span, 2 * width :] = acc[0:128, span].T.astype(BF16)

    partner = ctx_peers[2]
    across = me + 1 - 2 * lax.rem(me, 2)
    up = lax.rem(me + 2, GROUP)
    down = lax.rem(me + GROUP - 2, GROUP)
    onward = lax.rem(me + 2 + core * 4, GROUP)
    origin = lax.rem(me + 6 - core * 4, GROUP)

    def other(h):
        return h + 1 - 2 * lax.rem(h, 2)

    far = lax.rem(me + 4, GROUP)
    part = pl.ds(pl.multiple_of(core * (inner // 2), 128), inner // 2)
    rest_part = pl.ds(pl.multiple_of((1 - core) * (inner // 2), 128), inner // 2)
    mine_half = wout.at[part, :]
    sources = [across, down, up, other(down), other(up), far, other(far)]

    def slot_copy(src, k, source_here, ctx_to, head_to, send_index):
        return remote(src, wo.at[source_here, part], wsend.at[send_index], wrecv.at[k], ctx_to, head_to)

    w1 = [
        slot_copy(mine_half, 0, me, ctx, across, 0),
        slot_copy(mine_half, 1, me, ctx, up, 1),
        slot_copy(mine_half, 2, me, ctx, down, 2),
    ]
    w2 = [
        slot_copy(wo.at[across, part], 3, across, ctx, up, 3),
        slot_copy(wo.at[across, part], 4, across, ctx, down, 4),
    ]
    w3 = [
        slot_copy(wo.at[origin, part], 5, origin, ctx, onward, 5),
        slot_copy(wo.at[other(origin), part], 6, other(origin), ctx, onward, 6),
    ]
    w4 = [
        remote(wo.at[h, part], wo.at[h, part], wsend.at[7 + k], wrecv.at[7 + k], partner, me)
        for k, h in enumerate(sources)
    ]

    def arrived(k):
        remote(mine_half, wo.at[sources[k], part], wsend.at[0], wrecv.at[k], ctx, me).wait_recv()

    def partner_arrived(k):
        h = sources[k]
        remote(wo.at[h, part], wo.at[h, rest_part], wsend.at[0], wrecv.at[7 + k], partner, me).wait_recv()

    def first_rows():
        return [
            remote(
                st.at[0, blocks, :, pl.ds(0, 8), :], st.at[0, 0, :, pl.ds(0, 8), :],
                halo_send.at[0], halo_recv.at[0], ctx_peers[0], me,
            ),
            remote(
                st.at[1, 0, :, pl.ds(BLOCK, 8), :], st.at[1, blocks, :, pl.ds(BLOCK, 8), :],
                halo_send.at[1], halo_recv.at[1], ctx_peers[1], me,
            ),
        ]

    def map_rows():
        return [
            remote(
                sc.at[0, blocks, pl.ds(0, 8), :], sc.at[0, 0, pl.ds(0, 8), :],
                halo_send.at[2], halo_recv.at[2], ctx_peers[0], me,
            ),
            remote(
                sc.at[1, 0, pl.ds(BLOCK, 8), :], sc.at[1, blocks, pl.ds(BLOCK, 8), :],
                halo_send.at[3], halo_recv.at[3], ctx_peers[1], me,
            ),
        ]

    def convolve(source, shape_taps, s):
        total = None
        for k in range(4):
            shift = 5 + k if s == 0 else 3 - k
            term = shape_taps[k : k + 1, :] * source[shift : shift + BLOCK, :]
            total = term if total is None else total + term
        return silu(total)

    def project(i, carry):
        b = lax.rem(i + blocks - 1, blocks)
        load(b).wait()
        h = hbuf[b]
        hf = h.astype(F32)
        scale = lax.rsqrt(jnp.sum(hf * hf, axis=1, keepdims=True) / h.shape[1] + epsilon)
        p = dot(h, wX[...])
        ahead = p[:, :width] * scale
        behind = p[:, width : 2 * width] * scale
        for t in range(width // 128):
            at = slice(t * 128, (t + 1) * 128)
            st[0, b, t, 8:, :] = ahead[:, at]
            st[0, b + 1, t, 0:8, :] = ahead[BLOCK - 8 :, at]
            st[1, b + 1, t, :BLOCK, :] = behind[:, at]
            st[1, b, t, BLOCK:, :] = behind[0:8, at]
        dtb[b] = softplus(p[:, 2 * width :] * scale + bias)
        scl[b] = jnp.broadcast_to(scale, (BLOCK, 128))

        @pl.when(i == 2)
        def _():
            pl.semaphore_wait(barrier, len(ctx_peers) + len(head_peers))
            for copy in first_rows() + w1:
                copy.start()

        return carry

    lax.fori_loop(0, blocks, project, 0)

    for copy in first_rows():
        copy.wait_recv()
    st[0, 0, :, 0:8, :] = jnp.where(ctx == 0, 0.0, st[0, 0, :, 0:8, :])
    st[1, blocks, :, BLOCK:, :] = jnp.where(ctx == CTX - 1, 0.0, st[1, blocks, :, BLOCK:, :])

    state[...] = jnp.zeros_like(state)
    arow[...] = jnp.ones_like(arow)

    def local(i, carry):
        @pl.when(i == 4)
        def _():
            arrived(0)
            for copy in w2 + w4[:1]:
                copy.start()

        for s in range(2):
            b = i if s == 0 else blocks - 1 - i
            x = jnp.concatenate(
                [
                    convolve(st.at[s, b + s, t], conv_x[:, t * 128 : (t + 1) * 128], s)
                    for t in range(inner // 128)
                ],
                axis=1,
            )
            bt = convolve(st.at[s, b + s, inner // 128], conv_bc[:, :STATE], s).T.astype(BF16)
            btb[s, b] = bt
            vb[s, b] = x.astype(BF16)
            dt = dtb[b]
            high, rest = halves(dt * rate)
            tri = low[...] if s == 0 else upp[...]
            c = dot(tri, high) + dot(tri, rest)
            cum[s, b] = c
            end = c[BLOCK - 1 : BLOCK, :] if s == 0 else c[0:1, :]
            table = spread[s]
            late = dot(jnp.concatenate(halves(dt * jnp.exp2(end - c)), axis=1), table)
            decay = dot(
                jnp.concatenate(halves(jnp.broadcast_to(jnp.exp2(end), (16, 128))), axis=1), table
            )[0:1, :]
            ends = dot(bt, (x * late).astype(BF16))
            held = state[s]
            ent[s, b] = held
            state[s] = decay * held + ends
            before = arow[s, 0:1, :]
            prow[s, b] = jnp.broadcast_to(before, (8, inner))
            arow[s] = jnp.broadcast_to(before * decay, (8, inner))
        return carry

    lax.fori_loop(0, blocks, local, 0)

    xs[...] = jnp.zeros_like(xs)
    xa[...] = jnp.ones_like(xa)

    half = pl.ds(pl.multiple_of(core * 128, 128), 128)
    other_half = pl.ds(pl.multiple_of((1 - core) * 128, 128), 128)

    def packed(row):
        line = lax.broadcasted_iota(jnp.int32, (16, row.shape[1]), 0)
        high, rest = halves(row)
        return jnp.where(
            line == 0, high.astype(F32), jnp.where(line == 1, rest.astype(F32), 0.0)
        ).astype(BF16)

    def unpacked(tail):
        tail = tail.astype(F32)
        return tail[0:1, :] + tail[1:2, :]

    def joined(k, s, theirs, factor, now, now_a, before, before_a):
        earlier = lax.rem(lax.div(ctx, 2**k), 2) == 1 - s
        mine, reach = now_a[s, 0:1, :], before_a[s, 0:1, :]
        state_now = now[s]
        before[s] = jnp.where(earlier, reach * theirs + before[s], before[s])
        before_a[s] = jnp.broadcast_to(
            jnp.where(earlier, reach * factor, reach), before_a.shape[1:]
        )
        now[s] = jnp.where(earlier, mine * theirs + state_now, factor * state_now + theirs)
        now_a[s] = jnp.broadcast_to(mine * factor, now_a.shape[1:])

    place = lax.div(ctx, 4)
    swap = remote(msg, rmsg, ssend.at[0], srecv.at[0], ctx_peers[2], me)
    pairs = remote(hmsg.at[0], hrmsg.at[0], ssend.at[1], srecv.at[1], ctx_peers[3], me)
    along = [
        remote(
            hmsg.at[1, lax.div(place + d, 4)], xmsg.at[d - 1],
            ssend.at[1 + d], srecv.at[1 + d], ctx_peers[3 + d], me,
        )
        for d in range(1, 4)
    ]
    give = remote(fmsg, frmsg, ssend.at[5], srecv.at[5], ctx_peers[2], me)

    for s in range(2):
        msg[s, :STATE, :] = state[s].astype(BF16)
        msg[s, STATE:, :] = packed(arow[s, 0:1, :])
    swap.start()

    def fill_half(k):
        for s in range(2):
            hmsg[k, s, :STATE, :] = hs[s].astype(BF16)
            hmsg[k, s, STATE:, :] = packed(ha[s, 0:1, :])

    def merge_swap():
        swap.wait_recv()
        for s in range(2):
            theirs = rmsg[s, :STATE, :].astype(F32)
            joined(0, s, theirs, unpacked(rmsg[s, STATE:, :]), state, arow, xs, xa)
            hs[s] = state[s, :, half]
            ha[s] = arow[s, :, half]
        ys[...] = jnp.zeros_like(ys)
        ya[...] = jnp.ones_like(ya)
        fill_half(0)
        pairs.start()

    def merge_pairs():
        pairs.wait_recv()
        for s in range(2):
            theirs = hrmsg[0, s, :STATE, :].astype(F32)
            joined(1, s, theirs, unpacked(hrmsg[0, s, STATE:, :]), hs, ha, ys, ya)
        fill_half(1)
        for copy in along:
            copy.start()

    def merge_along():
        for copy in along:
            copy.wait_recv()
        for s in range(2):
            far_state = jnp.zeros((STATE, 128), F32)
            for d in (3, 2, 1) if s == 0 else (1, 2, 3):
                used = place >= d if s == 0 else place < d
                factor = unpacked(xmsg[d - 1, STATE:, :])
                theirs = xmsg[d - 1, :STATE, :].astype(F32)
                far_state = jnp.where(used, factor * far_state + theirs, far_state)
            ys[s] = ya[s, 0:1, :] * far_state + ys[s]
        fmsg[...] = ys[...].astype(BF16)
        give.start()

    def merge_give():
        give.wait_recv()
        for s in range(2):
            xs[s, :, half] = xa[s, 0:1, half] * ys[s] + xs[s, :, half]
            xs[s, :, other_half] = (
                xa[s, 0:1, other_half] * frmsg[s].astype(F32) + xs[s, :, other_half]
            )

    def project_maps(i, carry):
        b = lax.rem(i + blocks - 1, blocks)
        p = dot(hbuf[b], wC[...])
        scale = scl[b]
        ahead = p[:, :STATE] * scale
        sc[0, b, 8:, :] = ahead
        sc[0, b + 1, 0:8, :] = ahead[BLOCK - 8 :, :]
        behind = p[:, STATE:] * scale
        sc[1, b + 1, :BLOCK, :] = behind
        sc[1, b, BLOCK:, :] = behind[0:8, :]

        @pl.when(i == 2)
        def _():
            for copy in map_rows():
                copy.start()

        return carry

    lax.fori_loop(0, blocks, project_maps, 0)

    def within(step, carry):
        i = lax.rem(step + 1, blocks)

        @pl.when(step == 0)
        def _():
            merge_swap()

        @pl.when(step == 1)
        def _():
            for k in range(1, 5):
                arrived(k)
            for copy in w3 + w4[1:5]:
                copy.start()

        @pl.when(step == 3)
        def _():
            merge_pairs()

        @pl.when(step == blocks - 2)
        def _():
            for copy in map_rows():
                copy.wait_recv()
            sc[0, 0, 0:8, :] = jnp.where(ctx == 0, 0.0, sc[0, 0, 0:8, :])
            sc[1, blocks, BLOCK:, :] = jnp.where(ctx == CTX - 1, 0.0, sc[1, blocks, BLOCK:, :])

        dt_pair = jnp.concatenate(halves(dtb[i]), axis=1)
        first, second = iotas((128, 128))
        side = second < HEAD
        for s in range(2):
            c = cum[s, i]
            maps = convolve(sc.at[s, i + s], conv_bc[:, STATE:], s).astype(BF16)
            cb[s, i] = maps
            ec[s, i] = dot(jnp.concatenate(halves(jnp.exp2(c)), axis=1), spread[s])
            weighted = (vb[s, i].astype(F32) * dot(dt_pair, spread[s])).astype(BF16)
            keep = first >= second if s == 0 else first <= second
            scores = dot(maps, btb[s, i])
            corner = [
                jnp.where(keep, scores[:128, :128], 0.0),
                jnp.where(keep, scores[128:, 128:], 0.0),
            ]
            cross = scores[128:, :128] if s == 0 else scores[:128, 128:]
            turned = c.T
            for pair in range(heads // 2):
                at = slice(pair * 128, (pair + 1) * 128)
                short, long = [], []
                for t in range(2):
                    lane = s * heads + pair * 2 + t
                    down_col = [c[:128, lane : lane + 1], c[128:, lane : lane + 1]]
                    row = turned[lane : lane + 1, :]
                    over = [row[:, :128], row[:, 128:]]
                    square = [
                        (corner[q] * jnp.exp2(jnp.minimum(down_col[q] - over[q], 0.0))).astype(BF16)
                        for q in range(2)
                    ]
                    far_off = (cross * jnp.exp2(down_col[1 - s] - over[s])).astype(BF16)
                    short.append(square[s])
                    long.extend([far_off, square[1]] if s == 0 else [square[0], far_off])
                w = weighted[:, at]
                w_rows = [w[:128, :], w[128:, :]]
                zero = jnp.zeros_like(w_rows[0])
                first_head = [jnp.where(side, v, zero) for v in w_rows]
                second_head = [jnp.where(side, zero, v) for v in w_rows]
                brief = dot(
                    jnp.concatenate(short, axis=1),
                    jnp.concatenate([first_head[s], second_head[s]], axis=0),
                )
                full = dot(
                    jnp.concatenate(long, axis=1), jnp.concatenate(first_head + second_head, axis=0)
                )
                result = [brief, full] if s == 0 else [full, brief]
                for q in range(2):
                    down_rows = slice(q * 128, (q + 1) * 128)
                    ins[s, i, down_rows, at] = result[q] + skips[0:1, at] * vb[
                        s, i, down_rows, at
                    ].astype(F32)
        return carry

    lax.fori_loop(0, blocks, within, 0)
    merge_along()
    merge_give()

    def finish(i, carry):
        b = lax.rem(me + 1 + i, blocks)
        both = jnp.zeros((BLOCK, inner), F32)
        scale = jnp.concatenate([scl[b]] * (inner // 128), axis=1)
        h = hbuf[b]
        for s in range(2):
            gate = silu(dot(h, wZ[:, s * inner : (s + 1) * inner]) * scale)
            whole = (ent[s, b] + prow[s, b][0:1, :] * xs[s]).astype(BF16)
            result = ins[s, b] + ec[s, b] * dot(cb[s, b], whole)
            gated = result * gate
            power = dot((gated * gated).astype(BF16), mean[...])
            both = both + gated * lax.rsqrt(power + epsilon)
        cbuf[b] = both.astype(BF16)

        @pl.when(i == 2)
        def _():
            for k in (5, 6):
                arrived(k)
            for copy in w4[5:]:
                copy.start()

        @pl.when(i < blocks - 1)
        def _():
            remote(cbuf.at[b], rbuf.at[me], csend.at[b], crecv.at[me], ctx, b).start()

        return carry

    lax.fori_loop(0, blocks, finish, 0)

    own.wait()
    for k in range(7):
        partner_arrived(k)

    acc[...] = hbuf[me].astype(F32)

    def multiply(block, j):
        acc[...] += dot(block, wo[j])

    multiply(cbuf[me], me)

    def gathered(i, carry):
        j = lax.rem(me + blocks - 1 - i, blocks)
        remote(cbuf.at[j], rbuf.at[j], csend.at[j], crecv.at[j], ctx, j).wait_recv()
        multiply(rbuf[j], j)
        return carry

    lax.fori_loop(0, blocks - 1, gathered, 0)
    out[...] = acc[...].astype(BF16)

    for copy in w1 + w2 + w3 + w4 + first_rows() + map_rows() + [swap, pairs, give] + along:
        copy.wait_send()

    def drained(i, carry):
        j = lax.rem(me + 1 + i, blocks)
        remote(cbuf.at[j], rbuf.at[me], csend.at[j], crecv.at[me], ctx, j).wait_send()
        return carry

    lax.fori_loop(0, blocks - 1, drained, 0)


def on_device(
    hidden, norm_gain, w_zx, w_bc, w_dt, dt_bias, decay_rate, skip_gain, conv_x, conv_bc, w_out
):
    amount, wide = hidden.shape
    inner = conv_x.shape[1]
    heads = w_dt.shape[1]
    width = inner + STATE
    blocks = amount // BLOCK
    vmem = pl.BlockSpec(memory_space=pltpu.VMEM)
    hbm = pl.BlockSpec(memory_space=pl.ANY)
    smem = pl.BlockSpec(memory_space=pltpu.SMEM)
    dma = pltpu.SemaphoreType.DMA
    return pl.pallas_call(
        kernel,
        out_shape=jax.ShapeDtypeStruct((BLOCK, wide), BF16),
        in_specs=[hbm, vmem, hbm, hbm, vmem, smem, smem, smem, vmem, vmem, hbm],
        out_specs=vmem,
        scratch_shapes=[
            pltpu.VMEM((blocks, BLOCK, wide), BF16),
            pltpu.VMEM((wide, 2 * width + 128), BF16),
            pltpu.VMEM((wide, 2 * inner), BF16),
            pltpu.VMEM((GROUP, inner, wide), BF16),
            pltpu.VMEM((2, blocks + 1, width // 128, BLOCK + 8, 128), F32),
            pltpu.VMEM((blocks, BLOCK, 128), F32),
            pltpu.VMEM((blocks, BLOCK, 128), F32),
            pltpu.VMEM((2, blocks, BLOCK, inner), BF16),
            pltpu.VMEM((2, blocks, STATE, BLOCK), BF16),
            pltpu.VMEM((2, blocks, BLOCK, STATE), BF16),
            pltpu.VMEM((2, blocks, BLOCK, 128), F32),
            pltpu.VMEM((2, blocks, BLOCK, inner), F32),
            pltpu.VMEM((2, blocks, STATE, inner), F32),
            pltpu.VMEM((2, blocks, 8, inner), F32),
            pltpu.VMEM((2, blocks, BLOCK, inner), F32),
            pltpu.VMEM((2, STATE, inner), F32),
            pltpu.VMEM((2, 8, inner), F32),
            pltpu.VMEM((2, STATE, inner), F32),
            pltpu.VMEM((2, 8, inner), F32),
            pltpu.VMEM((2, MESSAGE, inner), BF16),
            pltpu.VMEM((2, MESSAGE, inner), BF16),
            pltpu.VMEM((GROUP, BLOCK, inner), BF16),
            pltpu.VMEM((GROUP, BLOCK, inner), BF16),
            pltpu.VMEM((BLOCK, wide), F32),
            pltpu.VMEM((BLOCK, BLOCK), BF16),
            pltpu.VMEM((BLOCK, BLOCK), BF16),
            pltpu.VMEM((2, BLOCK, BLOCK), BF16),
            pltpu.VMEM((BLOCK, BLOCK), BF16),
            pltpu.VMEM((BLOCK, BLOCK), BF16),
            pltpu.VMEM((wide, 2 * inner), BF16),
            pltpu.VMEM((wide, 2 * STATE), BF16),
            pltpu.VMEM((8, inner), F32),
            pltpu.VMEM((wide, 2 * STATE), BF16),
            pltpu.VMEM((2, blocks + 1, BLOCK + 8, STATE), F32),
            pltpu.VMEM((2, STATE, 128), F32),
            pltpu.VMEM((2, 8, 128), F32),
            pltpu.VMEM((2, STATE, 128), F32),
            pltpu.VMEM((2, 8, 128), F32),
            pltpu.VMEM((2, 2, MESSAGE, 128), BF16),
            pltpu.VMEM((1, 2, MESSAGE, 128), BF16),
            pltpu.VMEM((3, MESSAGE, 128), BF16),
            pltpu.VMEM((2, STATE, 128), BF16),
            pltpu.VMEM((2, STATE, 128), BF16),
            dma((2,)),
            dma((blocks,)),
            dma((1,)),
            dma((14,)),
            dma((14,)),
            dma((4,)),
            dma((4,)),
            dma((6,)),
            dma((6,)),
            dma((GROUP,)),
            dma((GROUP,)),
        ],
        compiler_params=pltpu.CompilerParams(
            collective_id=0, has_side_effects=True, vmem_limit_bytes=63 * 1024 * 1024
        ),
    )(
        hidden,
        norm_gain.reshape(8, wide // 8),
        w_zx.reshape(wide, 2 * inner),
        w_bc,
        w_dt.T,
        dt_bias,
        decay_rate,
        skip_gain,
        conv_x,
        conv_bc,
        w_out,
    )


def solution(mesh):
    placed = (
        P("ctx", None),
        P(),
        P(None, None, "head"),
        P(),
        P(None, "head"),
        P("head"),
        P("head"),
        P("head"),
        P(None, "head"),
        P(),
        P("head", None),
    )
    return jax.shard_map(
        on_device, mesh=mesh, in_specs=placed, out_specs=P(("ctx", "head"), None), check_vma=False
    )
```

time: 73.6 us -> 60.6 us (0.82)
  the two profiles are of different devices: /device:TPU:0 before, /device:TPU:1 now
where the time goes in v1:
time: 60.6 us; the launch traced here: 60.3 us
  Pallas kernels  56 us (92%)
  local copies, waits for them, and re-layouts  4.31 us (7%)
    pallas_call x1, Pallas kernels, on_device(): pl.pallas_call(kernel, out_shape=jax.ShapeDtypeStruct((BLOCK, wide), BF16...  56 us
    unnamed x2, local copies, waits for them, and re-layouts  4.31 us

profile of v1, /device:TPU:1, one launch (start us, length us, event | category | flops | bytes accessed | tf_op | source)
XLA Modules:
  0.0 60.3 jit_solution(5880651652633765694)
XLA Ops:
  0.0 2.4 %copy.12 = bf16[128,8,2,256]{3,1,2,0:T(8,128)(2,1)} copy(bf16[128,8,2,256]{3,2,1,0:T(2,128)(2,1)} %bitcast.5) | data formatting | bytes 2097152
  2.4 56.0 %shard_map.109 = bf16[256,1024]{1,0:T(8,128)(2,1)} custom-call(bf16[2048,1024]{1,0:T(8,128)(2,1)} %hid.1, f32[8,128]{1,0:T(8,128)} %bitcast.7, bf16[1024,512]{1,0:T(8,128)(2,1)} %bitcast.4, bf16[1024,256]{1,0:T(8,128)(2,1)} %wbc_hbm.1, bf16[4,1024]{1,0:T(4,128)(2,1)} %bitcast.6, f32[4]{0:T(128)} %bias_in.1, f32[4]{0:T(128)} %rate_in.1, f32[4]{0:T(128)} %skip_in.1, ...), custom_call_target="tpu_custom_call" | custom-call | tf_op jit(solution)/shard_map/pallas_call | solution.py:569
  58.5 1.9 %copy.14 = bf16[256,1024]{1,0:T(8,128)(2,1)} copy(bf16[256,1024]{1,0:T(8,128)(2,1)} %shard_map.109) | data formatting | bytes 1048576

commit v2 on v1

--- a/solution.py
+++ b/solution.py
@@ -52,9 +52,9 @@
 
 
 def kernel(
-    hid, gain, wzx_hbm, wbc_hbm, wdt, bias_in, rate_in, skip_in, conv_x, conv_bc, wout, out,
-    hbuf, wX, wZ, wo, st, scl, dtb, vb, btb, cb, cum, ec, ent, prow, ins,
-    state, arow, xs, xa, msg, rmsg, cbuf, rbuf, acc, low, upp, spread, mean, flip, wzx, wbc, skips, wC, sc,
+    hid, gain, wzx, wbc_hbm, wdt, bias_in, rate_in, skip_in, conv_x, conv_bc, wout, out,
+    hbuf, wX, wZ, wo, st, scl, dtb, vb, btb, cb, cum, raw, lateb, endb, ec, ent, prow, ins,
+    state, arow, xs, xa, msg, rmsg, cbuf, rbuf, acc, low, upp, spread, mean, flip, wbc, skips, wC, sc,
     hs, ha, ys, ya, hmsg, hrmsg, xmsg, fmsg, frmsg, wsem, hsem, osem, wsend, wrecv, halo_send, halo_recv, ssend, srecv, csend, crecv,
 ):
     blocks = hbuf.shape[0]
@@ -83,8 +83,10 @@
         )
 
     weights = [
-        pltpu.make_async_copy(wzx_hbm, wzx, wsem.at[0]),
-        pltpu.make_async_copy(wbc_hbm, wbc, wsem.at[1]),
+        pltpu.make_async_copy(wbc_hbm.at[span, :], wbc.at[span, :], wsem.at[j])
+        for j, span in enumerate(
+            pl.ds(n * BLOCK, BLOCK) for n in range(wzx.shape[0] // BLOCK)
+        )
     ]
     for copy in weights:
         copy.start()
@@ -117,12 +119,10 @@
 
     acc[0:128, :] = jnp.zeros((128, acc.shape[1]), F32)
     pieces = wX.shape[0] // BLOCK
-    for copy in weights:
-        copy.wait()
-
     def prepare(j, carry):
         span = pl.ds(pl.multiple_of(j * BLOCK, BLOCK), BLOCK)
         back = pl.ds(pl.multiple_of((pieces - 1 - j) * BLOCK, BLOCK), BLOCK)
+        pltpu.make_async_copy(wbc_hbm.at[span, :], wbc.at[span, :], wsem.at[j]).wait()
         lines = [gain[pl.ds(2 * j + t, 1), :] for t in range(2)]
         column = jnp.concatenate(
             [jnp.broadcast_to(line, (128, 128)).T for line in lines], axis=0
@@ -219,9 +219,24 @@
         total = None
         for k in range(4):
             shift = 5 + k if s == 0 else 3 - k
-            term = shape_taps[k : k + 1, :] * source[shift : shift + BLOCK, :]
+            term = (0.5 * shape_taps[k : k + 1, :]) * source[shift : shift + BLOCK, :]
             total = term if total is None else total + term
-        return silu(total)
+        return total + total * jnp.tanh(total)
+
+    def settle(b):
+        dt = softplus(raw[b])
+        dtb[b] = dt
+        parts = jnp.concatenate(halves(dt * rate), axis=1)
+        ahead = dot(low[...], parts)
+        behind = dot(upp[...], parts)
+        forward = lax.broadcasted_iota(jnp.int32, (BLOCK, 128), 1) < heads
+        c = jnp.where(
+            forward, ahead[:, :128] + ahead[:, 128:], behind[:, :128] + behind[:, 128:]
+        )
+        cum[b] = c
+        end = jnp.where(forward[0:1, :], c[BLOCK - 1 : BLOCK, :], c[0:1, :])
+        lateb[b] = jnp.concatenate(halves(dt * jnp.exp2(end - c)), axis=1)
+        endb[b] = jnp.concatenate(halves(jnp.broadcast_to(jnp.exp2(end), (16, 128))), axis=1)
 
     def project(i, carry):
         b = lax.rem(i + blocks - 1, blocks)
@@ -229,19 +244,19 @@
         h = hbuf[b]
         hf = h.astype(F32)
         scale = lax.rsqrt(jnp.sum(hf * hf, axis=1, keepdims=True) / h.shape[1] + epsilon)
-        p = dot(h, wX[...])
-        ahead = p[:, :width] * scale
-        behind = p[:, width : 2 * width] * scale
+        ahead = dot(h, wX[:, :width]) * scale
+        p = dot(h, wX[:, width:])
+        behind = p[:, :width] * scale
         for t in range(width // 128):
             at = slice(t * 128, (t + 1) * 128)
             st[0, b, t, 8:, :] = ahead[:, at]
             st[0, b + 1, t, 0:8, :] = ahead[BLOCK - 8 :, at]
             st[1, b + 1, t, :BLOCK, :] = behind[:, at]
             st[1, b, t, BLOCK:, :] = behind[0:8, at]
-        dtb[b] = softplus(p[:, 2 * width :] * scale + bias)
+        raw[b] = p[:, width:] * scale + bias
         scl[b] = jnp.broadcast_to(scale, (BLOCK, 128))
 
-        @pl.when(i == 2)
+        @pl.when(i == 1)
         def _():
             pl.semaphore_wait(barrier, len(ctx_peers) + len(head_peers))
             for copy in first_rows() + w1:
@@ -250,6 +265,13 @@
         return carry
 
     lax.fori_loop(0, blocks, project, 0)
+
+    def settle_two(i, carry):
+        for u in range(4):
+            settle(4 * i + u)
+        return carry
+
+    lax.fori_loop(0, blocks // 4, settle_two, 0)
 
     for copy in first_rows():
         copy.wait_recv()
@@ -278,17 +300,8 @@
             bt = convolve(st.at[s, b + s, inner // 128], conv_bc[:, :STATE], s).T.astype(BF16)
             btb[s, b] = bt
             vb[s, b] = x.astype(BF16)
-            dt = dtb[b]
-            high, rest = halves(dt * rate)
-            tri = low[...] if s == 0 else upp[...]
-            c = dot(tri, high) + dot(tri, rest)
-            cum[s, b] = c
-            end = c[BLOCK - 1 : BLOCK, :] if s == 0 else c[0:1, :]
-            table = spread[s]
-            late = dot(jnp.concatenate(halves(dt * jnp.exp2(end - c)), axis=1), table)
-            decay = dot(
-                jnp.concatenate(halves(jnp.broadcast_to(jnp.exp2(end), (16, 128))), axis=1), table
-            )[0:1, :]
+            late = dot(lateb[b], spread[s])
+            decay = dot(endb[b], spread[s])[0:1, :]
             ends = dot(bt, (x * late).astype(BF16))
             held = state[s]
             ent[s, b] = held
@@ -409,6 +422,10 @@
             for copy in map_rows():
                 copy.start()
 
+        @pl.when(i == 6)
+        def _():
+            merge_swap()
+
         return carry
 
     lax.fori_loop(0, blocks, project_maps, 0)
@@ -416,11 +433,7 @@
     def within(step, carry):
         i = lax.rem(step + 1, blocks)
 
-        @pl.when(step == 0)
-        def _():
-            merge_swap()
-
-        @pl.when(step == 1)
+        @pl.when(step == 2)
         def _():
             for k in range(1, 5):
                 arrived(k)
@@ -442,7 +455,7 @@
         first, second = iotas((128, 128))
         side = second < HEAD
         for s in range(2):
-            c = cum[s, i]
+            c = cum[i]
             maps = convolve(sc.at[s, i + s], conv_bc[:, STATE:], s).astype(BF16)
             cb[s, i] = maps
             ec[s, i] = dot(jnp.concatenate(halves(jnp.exp2(c)), axis=1), spread[s])
@@ -568,8 +581,8 @@
     dma = pltpu.SemaphoreType.DMA
     return pl.pallas_call(
         kernel,
-        out_shape=jax.ShapeDtypeStruct((BLOCK, wide), BF16),
-        in_specs=[hbm, vmem, hbm, hbm, vmem, smem, smem, smem, vmem, vmem, hbm],
+        out_shape=pltpu.VMEM((BLOCK, wide), BF16),
+        in_specs=[hbm, vmem, vmem, hbm, vmem, smem, smem, smem, vmem, vmem, hbm],
         out_specs=vmem,
         scratch_shapes=[
             pltpu.VMEM((blocks, BLOCK, wide), BF16),
@@ -582,7 +595,10 @@
             pltpu.VMEM((2, blocks, BLOCK, inner), BF16),
             pltpu.VMEM((2, blocks, STATE, BLOCK), BF16),
             pltpu.VMEM((2, blocks, BLOCK, STATE), BF16),
-            pltpu.VMEM((2, blocks, BLOCK, 128), F32),
+            pltpu.VMEM((blocks, BLOCK, 128), F32),
+            pltpu.VMEM((blocks, BLOCK, 128), F32),
+            pltpu.VMEM((blocks, BLOCK, 256), BF16),
+            pltpu.VMEM((blocks, 16, 256), BF16),
             pltpu.VMEM((2, blocks, BLOCK, inner), F32),
             pltpu.VMEM((2, blocks, STATE, inner), F32),
             pltpu.VMEM((2, blocks, 8, inner), F32),
@@ -601,7 +617,6 @@
             pltpu.VMEM((2, BLOCK, BLOCK), BF16),
             pltpu.VMEM((BLOCK, BLOCK), BF16),
             pltpu.VMEM((BLOCK, BLOCK), BF16),
-            pltpu.VMEM((wide, 2 * inner), BF16),
             pltpu.VMEM((wide, 2 * STATE), BF16),
             pltpu.VMEM((8, inner), F32),
             pltpu.VMEM((wide, 2 * STATE), BF16),
@@ -615,7 +630,7 @@
             pltpu.VMEM((3, MESSAGE, 128), BF16),
             pltpu.VMEM((2, STATE, 128), BF16),
             pltpu.VMEM((2, STATE, 128), BF16),
-            dma((2,)),
+            dma((wide // BLOCK,)),
             dma((blocks,)),
             dma((1,)),
             dma((14,)),
@@ -628,12 +643,12 @@
             dma((GROUP,)),
         ],
         compiler_params=pltpu.CompilerParams(
-            collective_id=0, has_side_effects=True, vmem_limit_bytes=63 * 1024 * 1024
+            collective_id=0, has_side_effects=True, vmem_limit_bytes=56 * 1024 * 1024
         ),
     )(
         hidden,
         norm_gain.reshape(8, wide // 8),
-        w_zx.reshape(wide, 2 * inner),
+        pltpu.with_memory_space_constraint(w_zx.reshape(wide, 2 * inner), pltpu.VMEM),
         w_bc,
         w_dt.T,
         dt_bias,

time: 60.6 us -> 53.6 us (0.88)
  Pallas kernels: 56 us -> 51.2 us
  local copies, waits for them, and re-layouts: 4.31 us -> 2.24 us
    pallas_call x1, Pallas kernels: 56 us -> 51.2 us  [on_device(): pl.pallas_call(kernel, out_shape=pltpu.VMEM((BLOCK, wide), BF16), in_spec...]
    unnamed x2, local copies, waits for them, and re-layouts: 4.31 us -> 2.24 us
where the time goes in v2:
time: 53.6 us; the launch traced here: 53.4 us
  Pallas kernels  51.2 us (96%)
  local copies, waits for them, and re-layouts  2.24 us (4%)
    pallas_call x1, Pallas kernels, on_device(): pl.pallas_call(kernel, out_shape=pltpu.VMEM((BLOCK, wide), BF16), in_spec...  51.2 us
    unnamed x2, local copies, waits for them, and re-layouts  2.24 us

profile of v2, /device:TPU:1, one launch (start us, length us, event | category | flops | bytes accessed | tf_op | source)
XLA Modules:
  0.0 53.4 jit_solution(6451941453202222234)
XLA Ops:
  0.0 1.4 %copy.12 = bf16[128,8,2,256]{3,1,2,0:T(8,128)(2,1)S(1)} copy(bf16[128,8,2,256]{3,2,1,0:T(2,128)(2,1)} %bitcast.5) | data formatting | bytes 2097152
  1.5 51.2 %shard_map.109 = bf16[256,1024]{1,0:T(8,128)(2,1)S(1)} custom-call(bf16[2048,1024]{1,0:T(8,128)(2,1)} %hid.1, f32[8,128]{1,0:T(8,128)} %bitcast.7, bf16[1024,512]{1,0:T(8,128)(2,1)S(1)} %bitcast.4, bf16[1024,256]{1,0:T(8,128)(2,1)} %wbc_hbm.1, bf16[4,1024]{1,0:T(4,128)(2,1)} %bitcast.6, f32[4]{0:T(128)} %bias_in.1, f32[4]{0:T(128)} %rate_in.1, f32[4]{0:T(128)} %skip_in.1, ...), custom_call_target="tpu_custom_call" | custom-call | tf_op jit(solution)/shard_map/pallas_call | solution.py:582
  52.6 0.8 %copy.14 = bf16[256,1024]{1,0:T(8,128)(2,1)} copy(bf16[256,1024]{1,0:T(8,128)(2,1)S(1)} %shard_map.109) | data formatting | bytes 1048576

commit v3 on v2

--- a/solution.py
+++ b/solution.py
@@ -282,7 +282,7 @@
     arow[...] = jnp.ones_like(arow)
 
     def local(i, carry):
-        @pl.when(i == 4)
+        @pl.when(i == 6)
         def _():
             arrived(0)
             for copy in w2 + w4[:1]:
@@ -433,7 +433,7 @@
     def within(step, carry):
         i = lax.rem(step + 1, blocks)
 
-        @pl.when(step == 2)
+        @pl.when(step == 4)
         def _():
             for k in range(1, 5):
                 arrived(k)
@@ -521,7 +521,7 @@
             both = both + gated * lax.rsqrt(power + epsilon)
         cbuf[b] = both.astype(BF16)
 
-        @pl.when(i == 2)
+        @pl.when(i == 4)
         def _():
             for k in (5, 6):
                 arrived(k)

time: 53.6 us -> 53.1 us (level)
  no operation moved by 1% of the time
where the time goes in v3:
time: 53.1 us; the launch traced here: 52.9 us
  Pallas kernels  50.7 us (95%)
  local copies, waits for them, and re-layouts  2.24 us (4%)
    pallas_call x1, Pallas kernels, on_device(): pl.pallas_call(kernel, out_shape=pltpu.VMEM((BLOCK, wide), BF16), in_spec...  50.7 us
    unnamed x2, local copies, waits for them, and re-layouts  2.24 us

profile of v3, /device:TPU:1, one launch (start us, length us, event | category | flops | bytes accessed | tf_op | source)
XLA Modules:
  0.0 52.9 jit_solution(14160155414811749570)
XLA Ops:
  0.0 1.4 %copy.12 = bf16[128,8,2,256]{3,1,2,0:T(8,128)(2,1)S(1)} copy(bf16[128,8,2,256]{3,2,1,0:T(2,128)(2,1)} %bitcast.5) | data formatting | bytes 2097152
  1.5 50.7 %shard_map.109 = bf16[256,1024]{1,0:T(8,128)(2,1)S(1)} custom-call(bf16[2048,1024]{1,0:T(8,128)(2,1)} %hid.1, f32[8,128]{1,0:T(8,128)} %bitcast.7, bf16[1024,512]{1,0:T(8,128)(2,1)S(1)} %bitcast.4, bf16[1024,256]{1,0:T(8,128)(2,1)} %wbc_hbm.1, bf16[4,1024]{1,0:T(4,128)(2,1)} %bitcast.6, f32[4]{0:T(128)} %bias_in.1, f32[4]{0:T(128)} %rate_in.1, f32[4]{0:T(128)} %skip_in.1, ...), custom_call_target="tpu_custom_call" | custom-call | tf_op jit(solution)/shard_map/pallas_call | solution.py:582
  52.1 0.8 %copy.14 = bf16[256,1024]{1,0:T(8,128)(2,1)} copy(bf16[256,1024]{1,0:T(8,128)(2,1)S(1)} %shard_map.109) | data formatting | bytes 1048576

commit v4 on v3

--- a/solution.py
+++ b/solution.py
@@ -54,7 +54,7 @@
 def kernel(
     hid, gain, wzx, wbc_hbm, wdt, bias_in, rate_in, skip_in, conv_x, conv_bc, wout, out,
     hbuf, wX, wZ, wo, st, scl, dtb, vb, btb, cb, cum, raw, lateb, endb, ec, ent, prow, ins,
-    state, arow, xs, xa, msg, rmsg, cbuf, rbuf, acc, low, upp, spread, mean, flip, wbc, skips, wC, sc,
+    state, arow, xs, xa, msg, rmsg, cbuf, rbuf, acc, low, upp, spread, mean, flip, gates, wbc, skips, wC, sc,
     hs, ha, ys, ya, hmsg, hrmsg, xmsg, fmsg, frmsg, wsem, hsem, osem, wsend, wrecv, halo_send, halo_recv, ssend, srecv, csend, crecv,
 ):
     blocks = hbuf.shape[0]
@@ -504,19 +504,23 @@
         return carry
 
     lax.fori_loop(0, blocks, within, 0)
+    def make_gate(b, slot):
+        scale = jnp.concatenate([scl[b]] * (inner // 128), axis=1)
+        h = hbuf[b]
+        for s in range(2):
+            gates[slot, s] = silu(dot(h, wZ[:, s * inner : (s + 1) * inner]) * scale)
+
     merge_along()
+    make_gate(lax.rem(me + 1, blocks), 0)
     merge_give()
 
     def finish(i, carry):
         b = lax.rem(me + 1 + i, blocks)
         both = jnp.zeros((BLOCK, inner), F32)
-        scale = jnp.concatenate([scl[b]] * (inner // 128), axis=1)
-        h = hbuf[b]
-        for s in range(2):
-            gate = silu(dot(h, wZ[:, s * inner : (s + 1) * inner]) * scale)
+        for s in range(2):
             whole = (ent[s, b] + prow[s, b][0:1, :] * xs[s]).astype(BF16)
             result = ins[s, b] + ec[s, b] * dot(cb[s, b], whole)
-            gated = result * gate
+            gated = result * gates[lax.rem(i, 2), s]
             power = dot((gated * gated).astype(BF16), mean[...])
             both = both + gated * lax.rsqrt(power + epsilon)
         cbuf[b] = both.astype(BF16)
@@ -532,6 +536,7 @@
         def _():
             remote(cbuf.at[b], rbuf.at[me], csend.at[b], crecv.at[me], ctx, b).start()
 
+        make_gate(lax.rem(me + 2 + i, blocks), lax.rem(i + 1, 2))
         return carry
 
     lax.fori_loop(0, blocks, finish, 0)
@@ -617,6 +622,7 @@
             pltpu.VMEM((2, BLOCK, BLOCK), BF16),
             pltpu.VMEM((BLOCK, BLOCK), BF16),
             pltpu.VMEM((BLOCK, BLOCK), BF16),
+            pltpu.VMEM((2, 2, BLOCK, inner), F32),
             pltpu.VMEM((wide, 2 * STATE), BF16),
             pltpu.VMEM((8, inner), F32),
             pltpu.VMEM((wide, 2 * STATE), BF16),

time: 53.1 us -> 53.1 us (level)
  no operation moved by 1% of the time
where the time goes in v4:
time: 53.1 us; the launch traced here: 52.9 us
  Pallas kernels  50.6 us (95%)
  local copies, waits for them, and re-layouts  2.24 us (4%)
    pallas_call x1, Pallas kernels, on_device(): pl.pallas_call(kernel, out_shape=pltpu.VMEM((BLOCK, wide), BF16), in_spec...  50.6 us
    unnamed x2, local copies, waits for them, and re-layouts  2.24 us

profile of v4, /device:TPU:1, one launch (start us, length us, event | category | flops | bytes accessed | tf_op | source)
XLA Modules:
  0.0 52.9 jit_solution(18072795691272138985)
XLA Ops:
  0.0 1.4 %copy.12 = bf16[128,8,2,256]{3,1,2,0:T(8,128)(2,1)S(1)} copy(bf16[128,8,2,256]{3,2,1,0:T(2,128)(2,1)} %bitcast.5) | data formatting | bytes 2097152
  1.5 50.6 %shard_map.109 = bf16[256,1024]{1,0:T(8,128)(2,1)S(1)} custom-call(bf16[2048,1024]{1,0:T(8,128)(2,1)} %hid.1, f32[8,128]{1,0:T(8,128)} %bitcast.7, bf16[1024,512]{1,0:T(8,128)(2,1)S(1)} %bitcast.4, bf16[1024,256]{1,0:T(8,128)(2,1)} %wbc_hbm.1, bf16[4,1024]{1,0:T(4,128)(2,1)} %bitcast.6, f32[4]{0:T(128)} %bias_in.1, f32[4]{0:T(128)} %rate_in.1, f32[4]{0:T(128)} %skip_in.1, ...), custom_call_target="tpu_custom_call" | custom-call | tf_op jit(solution)/shard_map/pallas_call | solution.py:587
  52.1 0.8 %copy.14 = bf16[256,1024]{1,0:T(8,128)(2,1)} copy(bf16[256,1024]{1,0:T(8,128)(2,1)S(1)} %shard_map.109) | data formatting | bytes 1048576
